TPU v7x, 32 devices: a whole 2x2x4 slice. The times are simulated.
32 devices in a mesh: lat: 4 (over y, x), lon: 8 (over z, core).
Axes of the slice: x: 2, y: 2, z: 4, core: 2. Of those that a mesh axis runs over, the one named last changes fastest.
Arguments:
- field: float32 [80, 160, 384], P('lat', 'lon'), may hold values from -6 to 6
- lat_kernel: float32 [41], replicated, may hold values from 0.0121951215 to 0.036585364
- lon_kernel: float32 [41], replicated, may hold values from 0.0121951215 to 0.036585364
- time_taps: float32 [129], replicated, may hold values from -0.0058139535 to 0.0058139535
Outputs:
- basis: float32 [80, 160, 256], P('lat', 'lon')
- merged_factor: float32 [256, 256], replicated
All inputs are finite; a program needn't handle non-finite values.
Results may differ from a plain program's by a relative error of at most 0.00016.
Values sent between devices are 32-bit elements; how exact they have to be, the bound alone decides.
A program may use at most 64 MiB of HBM per device.

v0:
```python
import jax
import jax.numpy as jnp
from jax import lax
from jax.sharding import PartitionSpec as P

TH = 64
SH = 20


def extended_2(value, sides, width, wrap):
    for axis, dim in sides:
        peers, length = (lax.axis_size(axis), value.shape[dim])
        up = [(i, (i + 1) % peers) for i in range(peers if wrap else peers - 1)]
        down = [(j, i) for i, j in up]
        last = lax.slice_in_dim(value, length - width, length, axis=dim)
        initial = lax.slice_in_dim(value, 0, width, axis=dim)
        before = lax.ppermute(last, axis, up)
        after = lax.ppermute(initial, axis, down)
        value = jnp.concatenate([before, value, after], axis=dim)
    return value


def skewed(coeffs, count, width):
    period = jnp.pad(coeffs, (0, count))
    flat = jnp.tile(period, count)[: count * width]
    return flat.reshape(count, width)


def banded(kernel, count):
    return skewed(kernel, count, count + 2 * SH)


def smooth_rows(band, extended):
    rows_in, cols_in, hours = extended.shape
    flat = extended.reshape(rows_in, cols_in * hours)
    result = jnp.dot(
        band, flat, precision=lax.Precision.HIGHEST, preferred_element_type=jnp.float32
    )
    return result.reshape(band.shape[0], cols_in, hours)


def body(field, lat_kernel, lon_kernel, time_taps):
    rows_lat, rows_lon, length_in = field.shape
    steps_out = length_in - 2 * TH
    lat_place = lax.axis_index("lat")
    total_lat = rows_lat * lax.axis_size("lat")
    cells = total_lat * rows_lon * lax.axis_size("lon")
    centre = (jnp.arange(2 * TH + 1, dtype=jnp.int32) == TH).astype(jnp.float32)
    taps_full = time_taps + centre
    skew_time = skewed(taps_full, steps_out, length_in)
    filtered = lax.dot_general(
        field.reshape(-1, length_in),
        skew_time,
        (((1,), (1,)), ((), ())),
        precision=lax.Precision.HIGHEST,
        preferred_element_type=jnp.float32,
    ).reshape(rows_lat, rows_lon, steps_out)
    lat_band = banded(lat_kernel, rows_lat)
    lon_band = banded(lon_kernel, rows_lon)
    extended = extended_2(filtered, (("lat", 0),), SH, False)
    narrow = smooth_rows(lat_band, extended)
    lat_done = extended_2(narrow, (("lon", 1),), SH, True)
    smooth = jnp.einsum(
        "jk,ikt->ijt",
        lon_band,
        lat_done,
        precision=lax.Precision.HIGHEST,
        preferred_element_type=jnp.float32,
    )
    globrow = (lat_place * rows_lat + jnp.arange(rows_lat, dtype=jnp.int32)).astype(jnp.float32)
    latitude = jnp.pi * (globrow + 0.5) / total_lat - jnp.pi / 2
    weights = jnp.sqrt(jnp.cos(latitude))
    matrix = (smooth * weights[:, None, None]).reshape(-1, steps_out)
    local_gram = lax.dot_general(
        matrix,
        matrix,
        (((0,), (0,)), ((), ())),
        precision=lax.Precision.HIGHEST,
        preferred_element_type=jnp.float32,
    )
    gram = lax.psum(local_gram, ("lat", "lon"))
    lower = jnp.linalg.cholesky(gram)
    scale = jnp.sqrt(jnp.float32(cells))
    solved = lax.linalg.triangular_solve(
        lower, matrix, left_side=False, lower=True, transpose_a=True
    )
    basis = (solved * scale).reshape(rows_lat, rows_lon, steps_out)
    return (basis, lower.T / scale)


def solution(mesh):
    placed = (P("lat", "lon", None), P(), P(), P())
    return jax.shard_map(
        body, mesh=mesh, in_specs=placed, out_specs=(P("lat", "lon", None), P()), check_vma=False
    )
```

profile of v0, /device:TPU:0, one launch (start us, length us, event | category | flops | bytes accessed | tf_op | source)
XLA Modules:
  0.0 254.5 jit_solution(16534467174939067471)
XLA Ops:
  7.2 0.7 fusion.22
  8.0 0.5 tile.30
  8.6 0.4 copy-done
  9.1 0.8 convolution_bitcast_fusion
  10.0 4.9 %collective-permute-start = (f32[20,20,256]{2,1,0:T(8,128)S(1)}, f32[20,20,256]{2,1,0:T(8,128)S(1)}, u32[]{:S(2)}, u32[]{:S(2)}) collective-permute-start(f32[20,20,256]{2,1,0:T(8,128)S(1)} %reshape.66), channel_id=1, source_target_pairs={{0,8},{8,16},{16,24},{1,9},{9,17},{17,25},{2,10},{10,18},{18,26},{... | collective-permute-start | bytes 1228808 | tf_op jit(solution)/shard_map/ppermute | solution.py:17
  14.9 1.3 collective-permute-start.1
  16.5 8.8 %collective-permute-done = f32[20,20,256]{2,1,0:T(8,128)S(1)} collective-permute-done((f32[20,20,256]{2,1,0:T(8,128)S(1)}, f32[20,20,256]{2,1,0:T(8,128)S(1)}, u32[]{:S(2)}, u32[]{:S(2)}) %collective-permute-start) | collective-permute-done | bytes 409632 | tf_op jit(solution)/shard_map/ppermute | solution.py:17
  25.5 12.3 %collective-permute-done.1 = f32[20,20,256]{2,1,0:T(8,128)S(1)} collective-permute-done((f32[20,20,256]{2,1,0:T(8,128)S(1)}, f32[20,20,256]{2,1,0:T(8,128)S(1)}, u32[]{:S(2)}, u32[]{:S(2)}) %collective-permute-start.1) | collective-permute-done | bytes 409632 | tf_op jit(solution)/shard_map/ppermute | solution.py:18
  38.4 1.1 fusion.2
  39.5 3.5 %collective-permute-start.3 = (f32[20,20,256]{2,0,1:T(8,128)S(1)}, f32[20,20,256]{2,0,1:T(8,128)S(1)}, u32[]{:S(2)}, u32[]{:S(2)}) collective-permute-start(f32[20,20,256]{2,0,1:T(8,128)S(1)} %fusion.2), channel_id=1, source_target_pairs={{1,0},{2,1},{3,2},{4,3},{5,4},{6,5},{7,6},{0,7},{9,8},{10,9},{11,1... | collective-permute-start | bytes 1228808 | tf_op jit(solution)/shard_map/ppermute | solution.py:18
  43.3 9.4 %collective-permute-done.2 = f32[20,20,256]{2,0,1:T(8,128)S(1)} collective-permute-done((f32[20,20,256]{2,0,1:T(8,128)S(1)}, f32[20,20,256]{2,0,1:T(8,128)S(1)}, u32[]{:S(2)}, u32[]{:S(2)}) %collective-permute-start.2) | collective-permute-done | bytes 409632 | tf_op jit(solution)/shard_map/ppermute | solution.py:17
  52.8 1.2 fusion.7
  54.0 1.7 convolution_bitcast_fusion.1
  55.8 127.2 %all-reduce.6.cloned.1.call-done = f32[256,256]{0,1:T(8,128)} async-done(((f32[256,256]{0,1:T(8,128)}), f32[256,256]{0,1:T(8,128)}) %all-reduce.6.cloned.1.call-update) | async-done | bytes 262160 | tf_op jit(solution)/shard_map/psum | solution.py:81
  183.1 1.1 copy.14
  184.2 1.0 fusion.10
  185.2 11.7 %cholesky.50 = f32[128,128]{1,0:T(8,128)S(1)} custom-call(f32[128,128]{1,0:T(8,128)S(1)} %cholesky.118), custom_call_target="Cholesky" | custom-call | tf_op jit(solution)/shard_map/jit(cholesky)/cholesky | solution.py:82
  196.9 9.8 %custom-call.14 = f32[1,128,128]{1,2,0:T(8,128)S(1)} custom-call(f32[1,128,128]{2,1,0:T(8,128)S(1)} %get-tuple-element.29), custom_call_target="InvertDiagBlocksLowerTriangular" | custom-call | tf_op jit(solution)/shard_map/jit(cholesky)/cholesky | solution.py:82
  207.0 0.3 convolution_subtract_fusion
  207.2 11.9 %cholesky.105 = f32[128,128]{1,0:T(8,128)S(1)} custom-call(f32[128,128]{1,0:T(8,128)S(1)} %convolution_subtract_fusion), custom_call_target="Cholesky" | custom-call | tf_op jit(solution)/shard_map/jit(cholesky)/cholesky | solution.py:82
  219.1 0.7 compare_reduce_fusion
  221.3 4.0 %while.1 = (s32[]{:T(128)}, f32[256,256]{1,0:T(8,128)S(1)}, s32[2,2]{1,0:T(2,128)S(1)}, f32[2,128,128]{2,1,0:T(8,128)S(1)}, s32[]{:T(128)}) while((s32[]{:T(128)}, f32[256,256]{1,0:T(8,128)S(1)}, s32[2,2]{1,0:T(2,128)S(1)}, f32[2,128,128]{2,1,0:T(8,128)S(1)}, s32[]{:T(128)}) %tuple.30), condition=%wide.while_cond, body=%wide.while_body.sunk | while | flops 2 | bytes 131181 | solution.py:84
  221.3 0.6 fusion.35
  221.9 1.4 bitcast_dynamic-update-slice_fusion.2
  223.3 0.6 fusion.35
  223.8 1.4 bitcast_dynamic-update-slice_fusion.2
  225.2 19.7 %custom-call.15 = f32[2,128,128]{1,2,0:T(8,128)S(1)} custom-call(f32[2,128,128]{2,1,0:T(8,128)S(1)} %get-tuple-element.9), custom_call_target="InvertDiagBlocksLowerTriangular" | custom-call | tf_op jit(solution)/shard_map/triangular_solve | solution.py:84
  244.9 0.3 fusion.12
  245.2 0.3 slice_subtract_fusion
  245.6 0.3 fusion.14
  246.0 0.8 copy.16
  246.8 0.8 maximum_multiply_fusion
  (46 shorter events, 2.3 us)
Async XLA Ops:
  7.2 175.9 %all-reduce.6.cloned.1.call-start = ((), (), s32[]{:S(2)}) async-start(), calls=%async_computation | async-start | bytes 524288 | tf_op jit(solution)/shard_map/psum | solution.py:81
  7.9 1.1 copy-start
  9.1 7.2 %copy-start.1 = (f32[41]{0:T(128)S(1)}, f32[41]{0:T(128)}, u32[]{:S(2)}) copy-start(f32[41]{0:T(128)} %param.5) | copy-start | bytes 496
  10.0 15.3 %collective-permute-start = (f32[20,20,256]{2,1,0:T(8,128)S(1)}, f32[20,20,256]{2,1,0:T(8,128)S(1)}, u32[]{:S(2)}, u32[]{:S(2)}) collective-permute-start(f32[20,20,256]{2,1,0:T(8,128)S(1)} %reshape.66), channel_id=1, source_target_pairs={{0,8},{8,16},{16,24},{1,9},{9,17},{17,25},{2,10},{10,18},{18,26},{... | collective-permute-start | bytes 1228808 | tf_op jit(solution)/shard_map/ppermute | solution.py:17
  14.9 22.9 %collective-permute-start.1 = (f32[20,20,256]{2,1,0:T(8,128)S(1)}, f32[20,20,256]{2,1,0:T(8,128)S(1)}, u32[]{:S(2)}, u32[]{:S(2)}) collective-permute-start(f32[20,20,256]{2,1,0:T(8,128)S(1)} %reshape.66), channel_id=1, source_target_pairs={{8,0},{16,8},{24,16},{9,1},{17,9},{25,17},{10,2},{18,10},{26,18},{... | collective-permute-start | bytes 1228808 | tf_op jit(solution)/shard_map/ppermute | solution.py:18
  38.4 4.7 %copy-start.2 = (f32[41]{0:T(128)S(1)}, f32[41]{0:T(128)}, u32[]{:S(2)}) copy-start(f32[41]{0:T(128)} %param.6) | copy-start | bytes 496
  39.4 13.3 %collective-permute-start.2 = (f32[20,20,256]{2,0,1:T(8,128)S(1)}, f32[20,20,256]{2,0,1:T(8,128)S(1)}, u32[]{:S(2)}, u32[]{:S(2)}) collective-permute-start(f32[20,20,256]{2,0,1:T(8,128)S(1)} %fusion.2), channel_id=1, source_target_pairs={{0,1},{1,2},{2,3},{3,4},{4,5},{5,6},{6,7},{7,0},{8,9},{9,10},{10,1... | collective-permute-start | bytes 1228808 | tf_op jit(solution)/shard_map/ppermute | solution.py:17
  39.5 13.2 %collective-permute-start.3 = (f32[20,20,256]{2,0,1:T(8,128)S(1)}, f32[20,20,256]{2,0,1:T(8,128)S(1)}, u32[]{:S(2)}, u32[]{:S(2)}) collective-permute-start(f32[20,20,256]{2,0,1:T(8,128)S(1)} %fusion.2), channel_id=1, source_target_pairs={{1,0},{2,1},{3,2},{4,3},{5,4},{6,5},{7,6},{0,7},{9,8},{10,9},{11,1... | collective-permute-start | bytes 1228808 | tf_op jit(solution)/shard_map/ppermute | solution.py:18
Sparse Core Ops, SparseCore 0:
  55.9 127.1 all-reduce.5
where the time goes:
time: 255 us; the launch traced here: 254 us
  waiting for transfers between devices  158 us (62%)
  other arithmetic  56.7 us (22%)
  between operations  15.6 us (6%)
  starting transfers between devices  9.82 us (4%)
  local copies, waits for them, and re-layouts  8.32 us (3%)
  matrix products  6.27 us (2%)
    psum x1, waiting for transfers between devices, body(): gram = lax.psum(local_gram, ('lat', 'lon'))  127 us
    another operation x6, other arithmetic, body(): lower = jnp.linalg.cholesky(gram)  34.2 us
    another operation x2, other arithmetic, body(): lax.linalg.triangular_solve(lower, matrix, left_side=False, lower=True, t...  19.7 us
    ppermute x2, waiting for transfers between devices, extended_2(): before = lax.ppermute(last, axis, up)  18.2 us
    ppermute x2, waiting for transfers between devices, extended_2(): after = lax.ppermute(initial, axis, down)  12.3 us
  transfers between devices with their start and end apart: 5, of which 4 were waited for; matrix products, arithmetic and copies ran while one was open for 0% of the time, Pallas kernels for 0%

commit v1 on v0

--- a/solution.py
+++ b/solution.py
@@ -1,6 +1,10 @@
+import functools
+
 import jax
 import jax.numpy as jnp
 from jax import lax
+from jax.experimental import pallas as pl
+from jax.experimental.pallas import tpu as pltpu
 from jax.sharding import PartitionSpec as P
 
 TH = 64
@@ -37,6 +41,169 @@
         band, flat, precision=lax.Precision.HIGHEST, preferred_element_type=jnp.float32
     )
     return result.reshape(band.shape[0], cols_in, hours)
+
+
+MESH = pl.DeviceIdType.MESH
+NB = 32
+LANES = 128
+
+
+def sum_kernel(n_lat, n_lon, pair, g_ref, out_ref, rbuf, zbuf, ssem, rsem, zssem, zrsem, cssem, crsem):
+    lat, lon = lax.axis_index("lat"), lax.axis_index("lon")
+    n_p, n_z = n_lat * pair, n_lon // pair
+    rows = g_ref.shape[0] // n_p
+    core, z = lax.rem(lon, pair), lon // pair
+    me = lat * pair + core
+
+    def plane_peer(o):
+        peer = lax.rem(me + o, n_p)
+        return peer, (peer // pair, z * pair + lax.rem(peer, pair))
+
+    def z_peer(o):
+        return (lat, lax.rem(z + o, n_z) * pair + core)
+
+    barrier = pltpu.get_barrier_semaphore()
+    for o in range(1, n_p):
+        pl.semaphore_signal(barrier, inc=1, device_id=plane_peer(o)[1], device_id_type=MESH)
+    for o in range(1, n_z):
+        pl.semaphore_signal(barrier, inc=1, device_id=z_peer(o), device_id_type=MESH)
+    pl.semaphore_wait(barrier, n_p + n_z - 2)
+
+    copies = []
+    for o in range(1, n_p):
+        peer, dev = plane_peer(o)
+        c = pltpu.make_async_remote_copy(
+            src_ref=g_ref.at[pl.ds(pl.multiple_of(peer * rows, 8), rows)], dst_ref=rbuf.at[o],
+            send_sem=ssem.at[o], recv_sem=rsem.at[o], device_id=dev, device_id_type=MESH)
+        c.start()
+        copies.append(c)
+    mine = pl.ds(pl.multiple_of(me * rows, 8), rows)
+    acc = g_ref[mine, :]
+    for o in range(1, n_p):
+        copies[o - 1].wait_recv()
+        acc = acc + rbuf[o]
+    for c in copies:
+        c.wait_send()
+    zbuf[z] = acc
+
+    copies = []
+    for o in range(1, n_z):
+        c = pltpu.make_async_remote_copy(
+            src_ref=zbuf.at[z], dst_ref=zbuf.at[z],
+            send_sem=zssem.at[o], recv_sem=zrsem.at[o], device_id=z_peer(o), device_id_type=MESH)
+        c.start()
+        copies.append(c)
+    for c in copies:
+        c.wait()
+    total = zbuf[0]
+    for k in range(1, n_z):
+        total = total + zbuf[k]
+    out_ref[mine, :] = total
+
+    copies = []
+    for o in range(1, n_p):
+        c = pltpu.make_async_remote_copy(
+            src_ref=out_ref.at[mine], dst_ref=out_ref.at[mine],
+            send_sem=cssem.at[o], recv_sem=crsem.at[o], device_id=plane_peer(o)[1], device_id_type=MESH)
+        c.start()
+        copies.append(c)
+    for c in copies:
+        c.wait()
+
+
+def sum_over_mesh(gram):
+    n_lat, n_lon = lax.axis_size("lat"), lax.axis_size("lon")
+    pair = 2 if n_lon % 2 == 0 else 1
+    n_p, n_z = n_lat * pair, n_lon // pair
+    if gram.shape[0] % (8 * n_p):
+        return lax.psum(gram, ("lat", "lon"))
+    rows, width = gram.shape[0] // n_p, gram.shape[1]
+    dma = pltpu.SemaphoreType.DMA
+    return pl.pallas_call(
+        functools.partial(sum_kernel, n_lat, n_lon, pair),
+        out_shape=jax.ShapeDtypeStruct(gram.shape, jnp.float32),
+        in_specs=[pl.BlockSpec(memory_space=pltpu.VMEM)],
+        out_specs=pl.BlockSpec(memory_space=pltpu.VMEM),
+        scratch_shapes=[
+            pltpu.VMEM((n_p, rows, width), jnp.float32),
+            pltpu.VMEM((n_z, rows, width), jnp.float32),
+            dma((n_p,)), dma((n_p,)), dma((n_z,)), dma((n_z,)), dma((n_p,)), dma((n_p,)),
+        ],
+        compiler_params=pltpu.CompilerParams(collective_id=0, has_side_effects=True),
+        name="gram_sum",
+    )(gram)
+
+
+def factor_kernel(scale, g_ref, r_ref, y_ref, a, b):
+    n = g_ref.shape[0]
+    a[...] = g_ref[...]
+    b[...] = (lax.broadcasted_iota(jnp.int32, (n, n), 0) == lax.broadcasted_iota(jnp.int32, (n, n), 1)).astype(jnp.float32)
+    sub = lax.broadcasted_iota(jnp.int32, (8, LANES), 0)
+    tiles = n // LANES
+    for k in range(0, n, NB):
+        kt = k // LANES
+        live = [(a, t) for t in range(kt, tiles)] + [(b, t) for t in range(kt + 1)]
+        grp = [[ref[k + 8 * h:k + 8 * h + 8, t * LANES:(t + 1) * LANES] for ref, t in live] for h in range(NB // 8)]
+        for g in range(NB // 8):
+            hs = range(g, NB // 8)
+            lane = k + 8 * g - kt * LANES
+            cols = [{h: jnp.broadcast_to(grp[h][0][:, lane + q:lane + q + 1], (8, LANES)) for h in hs} for q in range(8)]
+            done = None
+            for q in range(8):
+                d = jnp.broadcast_to(cols[q][g][q:q + 1, :], (8, LANES))
+                inv = 1.0 / d
+                u = {h: cols[q][h] * inv for h in hs}
+                u[g] = jnp.where(sub > q, u[g], 0.0)
+                for p in range(q + 1, 8):
+                    e = jnp.broadcast_to(cols[p][g][q:q + 1, :], (8, LANES))
+                    for h in hs:
+                        cols[p][h] = cols[p][h] - u[h] * e
+                root = lax.sqrt(d)
+                done = root if done is None else jnp.where(sub == q, root, done)
+                for t in range(len(live)):
+                    row = jnp.broadcast_to(grp[g][t][q:q + 1, :], (8, LANES))
+                    for h in hs:
+                        grp[h][t] = grp[h][t] - u[h] * row
+            rinv = 1.0 / done
+            for t in range(len(live)):
+                grp[g][t] = grp[g][t] * rinv
+        panel = jnp.concatenate([jnp.concatenate(x, axis=1) for x in grp], axis=0)
+        n_a = tiles - kt
+        row_id = lax.broadcasted_iota(jnp.int32, (NB, n_a * LANES), 0) + k
+        lane_id = lax.broadcasted_iota(jnp.int32, (NB, n_a * LANES), 1) + kt * LANES
+        pa = panel[:, :n_a * LANES]
+        pb = panel[:, n_a * LANES:]
+        if kt:
+            r_ref[k:k + NB, :kt * LANES] = jnp.zeros((NB, kt * LANES), jnp.float32)
+        r_ref[k:k + NB, kt * LANES:] = jnp.where(lane_id >= row_id, pa / scale, 0.0)
+        y_ref[k:k + NB, :(kt + 1) * LANES] = pb * scale
+        if kt + 1 < tiles:
+            y_ref[k:k + NB, (kt + 1) * LANES:] = jnp.zeros((NB, n - (kt + 1) * LANES), jnp.float32)
+        nxt = k + NB
+        if nxt < n:
+            nt = nxt // LANES
+            left = panel[:, (nt - kt) * LANES:n_a * LANES]
+            dims = (((0,), (0,)), ((), ()))
+            right = panel[:, (nt - kt) * LANES:]
+            upd = lax.dot_general(left, right, dims, precision=lax.Precision.HIGHEST, preferred_element_type=jnp.float32)
+            upd = upd[nxt - nt * LANES:]
+            w_a = n - nt * LANES
+            a[nxt:, nt * LANES:] = a[nxt:, nt * LANES:] - upd[:, :w_a]
+            b[nxt:, :(kt + 1) * LANES] = b[nxt:, :(kt + 1) * LANES] - upd[:, w_a:]
+
+
+def factor(gram, scale):
+    n = gram.shape[0]
+    shape = jax.ShapeDtypeStruct((n, n), jnp.float32)
+    vmem = pl.BlockSpec(memory_space=pltpu.VMEM)
+    return pl.pallas_call(
+        functools.partial(factor_kernel, scale),
+        out_shape=(shape, shape),
+        in_specs=[vmem],
+        out_specs=(vmem, vmem),
+        scratch_shapes=[pltpu.VMEM((n, n), jnp.float32)] * 2,
+        name="factor",
+    )(gram)
 
 
 def body(field, lat_kernel, lon_kernel, time_taps):
@@ -78,14 +245,16 @@
         precision=lax.Precision.HIGHEST,
         preferred_element_type=jnp.float32,
     )
-    gram = lax.psum(local_gram, ("lat", "lon"))
-    lower = jnp.linalg.cholesky(gram)
-    scale = jnp.sqrt(jnp.float32(cells))
-    solved = lax.linalg.triangular_solve(
-        lower, matrix, left_side=False, lower=True, transpose_a=True
-    )
-    basis = (solved * scale).reshape(rows_lat, rows_lon, steps_out)
-    return (basis, lower.T / scale)
+    gram = sum_over_mesh(local_gram)
+    upper, inverse = factor(gram, float(cells) ** 0.5)
+    basis = lax.dot_general(
+        matrix,
+        inverse,
+        (((1,), (1,)), ((), ())),
+        precision=lax.Precision.HIGHEST,
+        preferred_element_type=jnp.float32,
+    ).reshape(rows_lat, rows_lon, steps_out)
+    return (basis, upper)
 
 
 def solution(mesh):

time: 255 us -> 81 us (0.32)
  waiting for transfers between devices: 158 us -> 19.2 us
  other arithmetic: 56.7 us -> 0.99 us
  Pallas kernels: 0 us -> 39.8 us
  between operations: 15.6 us -> 0.84 us
  local copies, waits for them, and re-layouts: 8.32 us -> 2.31 us
    psum x1 -> x0, waiting for transfers between devices: 127 us -> none  [body(): gram = lax.psum(local_gram, ('lat', 'lon'))]
    another operation x8 -> x0, other arithmetic: 53.9 us -> none  [the longest x6 34.2 us: body(): lower = jnp.linalg.cholesky(gram)]
    pallas_call x0 -> x2, Pallas kernels: none -> 39.8 us  [the longest x1 28.6 us: sum_over_mesh(): pl.pallas_call(functools.partial(sum_kernel, n_lat, n_lon, pair), out_sha...]
    ppermute x2, waiting for transfers between devices: 18.2 us -> 9.12 us  [extended_2(): before = lax.ppermute(last, axis, up)]
    another operation x11 -> x0, local copies, waits for them, and re-layouts: 4.06 us -> none
  transfers between devices with their start and end apart: 5 -> 4, of which waited for: 4 -> 4; matrix products, arithmetic and copies ran while one was open for 0% -> 1% of each run, Pallas kernels for 0% -> 0%
where the time goes in v1:
time: 81 us; the launch traced here: 80.7 us
  Pallas kernels  39.8 us (49%)
  waiting for transfers between devices  19.2 us (24%)
  starting transfers between devices  10.4 us (13%)
  matrix products  7.14 us (9%)
  local copies, waits for them, and re-layouts  2.31 us (3%)
  other arithmetic  0.99 us (1%)
  between operations  0.84 us (1%)
    pallas_call x1, Pallas kernels, sum_over_mesh(): pl.pallas_call(functools.partial(sum_kernel, n_lat, n_lon, pair), out_sha...  28.6 us
    pallas_call x1, Pallas kernels, factor(): pl.pallas_call(functools.partial(factor_kernel, scale), out_shape=(shape,...  11.3 us
    ppermute x2, waiting for transfers between devices, extended_2(): after = lax.ppermute(initial, axis, down)  10 us
    ppermute x2, waiting for transfers between devices, extended_2(): before = lax.ppermute(last, axis, up)  9.12 us
    ppermute x2, starting transfers between devices, extended_2(): before = lax.ppermute(last, axis, up)  5.59 us
    ppermute x2, starting transfers between devices, extended_2(): after = lax.ppermute(initial, axis, down)  4.82 us
    dot_general x1, matrix products, body(): lax.dot_general(matrix, inverse, (((1,), (1,)), ((), ())), precision=lax....  2.32 us
    dot_general x1, matrix products, body(): lax.dot_general(matrix, matrix, (((0,), (0,)), ((), ())), precision=lax.P...  1.73 us
  transfers between devices with their start and end apart: 4, of which 4 were waited for; matrix products, arithmetic and copies ran while one was open for 1% of the time, Pallas kernels for 0%

profile of v1, /device:TPU:0, one launch (start us, length us, event | category | flops | bytes accessed | tf_op | source)
XLA Modules:
  0.0 80.7 jit_solution(8414244851467723985)
XLA Ops:
  0.6 0.7 fusion.12
  1.3 0.1 tile.14
  1.4 0.5 tile.30
  1.9 0.1 reshape.44
  2.0 0.4 copy-done
  2.4 0.1 reshape.45
  2.5 0.0 copy-start.1
  2.5 0.8 %convolution_bitcast_fusion = f32[400,256]{1,0:T(8,128)S(1)} fusion(f32[256,384]{1,0:T(8,128)S(1)} %reshape.44, f32[400,384]{1,0:T(8,128)S(1)} %reshape.45), kind=kOutput, calls=%fused_computation.8 | convolution fusion | flops 471859200 | bytes 1417216 | tf_op jit(solution)/shard_map/dot_general | solution.py:218
  3.4 1.3 %collective-permute-start.1 = (f32[20,20,256]{2,1,0:T(8,128)S(1)}, f32[20,20,256]{2,1,0:T(8,128)S(1)}, u32[]{:S(2)}, u32[]{:S(2)}) collective-permute-start(f32[20,20,256]{2,1,0:T(8,128)S(1)} %reshape.46), channel_id=1, source_target_pairs={{8,0},{16,8},{24,16},{9,1},{17,9},{25,17},{10,2},{18,10},{26,18},{... | collective-permute-start | bytes 1228808 | tf_op jit(solution)/shard_map/ppermute | solution.py:22
  4.7 5.5 %collective-permute-start = (f32[20,20,256]{2,1,0:T(8,128)S(1)}, f32[20,20,256]{2,1,0:T(8,128)S(1)}, u32[]{:S(2)}, u32[]{:S(2)}) collective-permute-start(f32[20,20,256]{2,1,0:T(8,128)S(1)} %reshape.46), channel_id=1, source_target_pairs={{0,8},{8,16},{16,24},{1,9},{9,17},{17,25},{2,10},{10,18},{18,26},{... | collective-permute-start | bytes 1228808 | tf_op jit(solution)/shard_map/ppermute | solution.py:21
  10.2 0.1 concatenate.14
  10.4 0.1 tile.13
  10.5 0.1 reshape.48
  10.6 9.8 %collective-permute-done.1 = f32[20,20,256]{2,1,0:T(8,128)S(1)} collective-permute-done((f32[20,20,256]{2,1,0:T(8,128)S(1)}, f32[20,20,256]{2,1,0:T(8,128)S(1)}, u32[]{:S(2)}, u32[]{:S(2)}) %collective-permute-start.1) | collective-permute-done | bytes 409632 | tf_op jit(solution)/shard_map/ppermute | solution.py:22
  20.4 0.2 copy.10
  20.5 0.1 collective-permute-done
  20.7 0.2 copy.9
  20.9 0.2 maximum_bitcast_fusion
  21.0 0.2 dot_general.24
  21.3 1.1 %fusion.2 = f32[20,20,256]{2,0,1:T(8,128)S(1)} fusion(f32[20,60,1]{1,0,2:T(8,128)S(1)} %reshape.48, f32[20,256,60]{1,0,2:T(8,128)S(1)} %dot_general.24), kind=kOutput, calls=%fused_computation.4 | convolution fusion | flops 73728000 | bytes 1643200 | tf_op jit(solution)/shard_map/dot_general | solution.py:40
  22.3 0.1 collective-permute-start.2
  22.4 3.5 %collective-permute-start.3 = (f32[20,20,256]{2,0,1:T(8,128)S(1)}, f32[20,20,256]{2,0,1:T(8,128)S(1)}, u32[]{:S(2)}, u32[]{:S(2)}) collective-permute-start(f32[20,20,256]{2,0,1:T(8,128)S(1)} %fusion.2), channel_id=1, source_target_pairs={{1,0},{2,1},{3,2},{4,3},{5,4},{6,5},{7,6},{0,7},{9,8},{10,9},{11,1... | collective-permute-start | bytes 1228808 | tf_op jit(solution)/shard_map/ppermute | solution.py:22
  25.9 0.1 tile.32
  26.0 0.1 reshape.49
  26.2 9.0 %collective-permute-done.2 = f32[20,20,256]{2,0,1:T(8,128)S(1)} collective-permute-done((f32[20,20,256]{2,0,1:T(8,128)S(1)}, f32[20,20,256]{2,0,1:T(8,128)S(1)}, u32[]{:S(2)}, u32[]{:S(2)}) %collective-permute-start.2) | collective-permute-done | bytes 409632 | tf_op jit(solution)/shard_map/ppermute | solution.py:21
  35.2 0.3 collective-permute-done.3
  35.5 0.1 pad_maximum_fusion
  35.6 1.2 %fusion.7 = f32[20,20,256]{2,1,0:T(8,128)S(1)} fusion(f32[20,60,1]{1,0,2:T(8,128)S(1)} %reshape.49, f32[20,60,256]{2,0,1:T(8,128)S(1)} %pad_maximum_fusion, f32[20]{0:T(128)S(1)} %cosine_sqrt_fusion), kind=kOutput, calls=%fused_computation.7 | convolution fusion | flops 73830400 | bytes 1643280 | tf_op jit(solution)/shard_map/jk,ikt->ijt/dot_general | solution.py:230
  36.8 1.7 %convolution_bitcast_fusion.1.g_ref = f32[256,256]{1,0:T(8,128)} fusion(f32[20,20,256]{2,1,0:T(8,128)S(1)} %fusion.7), kind=kOutput, calls=%fused_computation.9 | convolution fusion | flops 314572800 | bytes 671744 | tf_op jit(solution)/shard_map/dot_general | solution.py:241
  38.5 28.6 %gram_sum.1.g_ref = f32[256,256]{1,0:T(8,128)} custom-call(f32[256,256]{1,0:T(8,128)} %convolution_bitcast_fusion.1.g_ref), custom_call_target="tpu_custom_call" | custom-call | tf_op jit(solution)/shard_map/gram_sum/pallas_call | solution.py:122
  67.1 11.3 %factor.1 = (f32[256,256]{1,0:T(8,128)}, f32[256,256]{1,0:T(8,128)}) custom-call(f32[256,256]{1,0:T(8,128)} %gram_sum.1.g_ref), custom_call_target="tpu_custom_call" | custom-call | tf_op jit(solution)/shard_map/factor/pallas_call | solution.py:199
  78.3 2.3 %fusion.10 = f32[20,20,256]{2,1,0:T(8,128)} fusion(f32[20,20,256]{2,1,0:T(8,128)S(1)} %fusion.7, f32[256,256]{1,0:T(8,128)} %get-tuple-element.4), kind=kOutput, calls=%fused_computation.10 | convolution fusion | flops 314572800 | bytes 1081344 | tf_op jit(solution)/shard_map/dot_general | solution.py:250
  (14 shorter events, 0.2 us)
Async XLA Ops:
  1.3 1.1 %copy-start = (f32[20,20,384]{2,1,0:T(8,128)S(1)}, f32[20,20,384]{2,1,0:T(8,128)}, u32[]{:S(2)}) copy-start(f32[20,20,384]{2,1,0:T(8,128)} %param.4) | copy-start | bytes 1843204
  2.5 7.9 %copy-start.1 = (f32[41]{0:T(128)S(1)}, f32[41]{0:T(128)}, u32[]{:S(2)}) copy-start(f32[41]{0:T(128)} %param.5) | copy-start | bytes 496
  3.4 16.9 %collective-permute-start.1 = (f32[20,20,256]{2,1,0:T(8,128)S(1)}, f32[20,20,256]{2,1,0:T(8,128)S(1)}, u32[]{:S(2)}, u32[]{:S(2)}) collective-permute-start(f32[20,20,256]{2,1,0:T(8,128)S(1)} %reshape.46), channel_id=1, source_target_pairs={{8,0},{16,8},{24,16},{9,1},{17,9},{25,17},{10,2},{18,10},{26,18},{... | collective-permute-start | bytes 1228808 | tf_op jit(solution)/shard_map/ppermute | solution.py:22
  4.7 16.0 %collective-permute-start = (f32[20,20,256]{2,1,0:T(8,128)S(1)}, f32[20,20,256]{2,1,0:T(8,128)S(1)}, u32[]{:S(2)}, u32[]{:S(2)}) collective-permute-start(f32[20,20,256]{2,1,0:T(8,128)S(1)} %reshape.46), channel_id=1, source_target_pairs={{0,8},{8,16},{16,24},{1,9},{9,17},{17,25},{2,10},{10,18},{18,26},{... | collective-permute-start | bytes 1228808 | tf_op jit(solution)/shard_map/ppermute | solution.py:21
  21.3 4.7 %copy-start.2 = (f32[41]{0:T(128)S(1)}, f32[41]{0:T(128)}, u32[]{:S(2)}) copy-start(f32[41]{0:T(128)} %param.6) | copy-start | bytes 496
  22.3 12.8 %collective-permute-start.2 = (f32[20,20,256]{2,0,1:T(8,128)S(1)}, f32[20,20,256]{2,0,1:T(8,128)S(1)}, u32[]{:S(2)}, u32[]{:S(2)}) collective-permute-start(f32[20,20,256]{2,0,1:T(8,128)S(1)} %fusion.2), channel_id=1, source_target_pairs={{0,1},{1,2},{2,3},{3,4},{4,5},{5,6},{6,7},{7,0},{8,9},{9,10},{10,1... | collective-permute-start | bytes 1228808 | tf_op jit(solution)/shard_map/ppermute | solution.py:21
  22.4 13.1 %collective-permute-start.3 = (f32[20,20,256]{2,0,1:T(8,128)S(1)}, f32[20,20,256]{2,0,1:T(8,128)S(1)}, u32[]{:S(2)}, u32[]{:S(2)}) collective-permute-start(f32[20,20,256]{2,0,1:T(8,128)S(1)} %fusion.2), channel_id=1, source_target_pairs={{1,0},{2,1},{3,2},{4,3},{5,4},{6,5},{7,6},{0,7},{9,8},{10,9},{11,1... | collective-permute-start | bytes 1228808 | tf_op jit(solution)/shard_map/ppermute | solution.py:22

commit v2 on v1

--- a/solution.py
+++ b/solution.py
@@ -11,36 +11,10 @@
 SH = 20
 
 
-def extended_2(value, sides, width, wrap):
-    for axis, dim in sides:
-        peers, length = (lax.axis_size(axis), value.shape[dim])
-        up = [(i, (i + 1) % peers) for i in range(peers if wrap else peers - 1)]
-        down = [(j, i) for i, j in up]
-        last = lax.slice_in_dim(value, length - width, length, axis=dim)
-        initial = lax.slice_in_dim(value, 0, width, axis=dim)
-        before = lax.ppermute(last, axis, up)
-        after = lax.ppermute(initial, axis, down)
-        value = jnp.concatenate([before, value, after], axis=dim)
-    return value
-
-
 def skewed(coeffs, count, width):
     period = jnp.pad(coeffs, (0, count))
     flat = jnp.tile(period, count)[: count * width]
     return flat.reshape(count, width)
-
-
-def banded(kernel, count):
-    return skewed(kernel, count, count + 2 * SH)
-
-
-def smooth_rows(band, extended):
-    rows_in, cols_in, hours = extended.shape
-    flat = extended.reshape(rows_in, cols_in * hours)
-    result = jnp.dot(
-        band, flat, precision=lax.Precision.HIGHEST, preferred_element_type=jnp.float32
-    )
-    return result.reshape(band.shape[0], cols_in, hours)
 
 
 MESH = pl.DeviceIdType.MESH
@@ -206,6 +180,190 @@
     )(gram)
 
 
+def halo_kernel(n_lat, n_lon, cols, taps, pieces, x_ref, w_ref, out_ref, ext, shifted, psend, precv, fsend, frecv, lsend, lrecv):
+    lat, lon = lax.axis_index("lat"), lax.axis_index("lon")
+    chunks, size = x_ref.shape[0], x_ref.shape[1]
+    odd = lax.rem(lat, 2)
+    partner = lat + 1 - 2 * odd
+    target = lat + 2 - 4 * odd
+    source = lat - 2 + 4 * odd
+    hands_on = jnp.logical_and(target >= 0, target < n_lat)
+    gets = jnp.logical_and(source >= 0, source < n_lat)
+    right, left = lax.rem(lon + 1, n_lon), lax.rem(lon + n_lon - 1, n_lon)
+    step = size // pieces
+
+    barrier = pltpu.get_barrier_semaphore()
+    for dev in ((partner, lon), (lat, left), (lat, right)):
+        pl.semaphore_signal(barrier, inc=1, device_id=dev, device_id_type=MESH)
+
+    @pl.when(gets)
+    def _():
+        pl.semaphore_signal(barrier, inc=1, device_id=(source, lon), device_id_type=MESH)
+
+    @pl.when(hands_on)
+    def _():
+        pl.semaphore_signal(barrier, inc=1, device_id=(target, lon), device_id_type=MESH)
+
+    pl.semaphore_wait(barrier, 3 + gets.astype(jnp.int32) + hands_on.astype(jnp.int32))
+
+    far = 2 * size * odd
+    near = 2 * size * (1 - odd)
+
+    def swap(c, s):
+        return pltpu.make_async_remote_copy(
+            src_ref=x_ref.at[c, pl.ds(s * step, step)],
+            dst_ref=ext.at[c, pl.ds(pl.multiple_of(far + s * step, 8), step)],
+            send_sem=psend.at[c, s], recv_sem=precv.at[c, s], device_id=(partner, lon), device_id_type=MESH)
+
+    def hand(c, s):
+        return pltpu.make_async_remote_copy(
+            src_ref=ext.at[c, pl.ds(pl.multiple_of(near + s * step, 8), step)],
+            dst_ref=ext.at[c, pl.ds(pl.multiple_of(far + s * step, 8), step)],
+            send_sem=fsend.at[c, s], recv_sem=frecv.at[c, s], device_id=(target, lon), device_id_type=MESH)
+
+    def side(c, way):
+        return pltpu.make_async_remote_copy(
+            src_ref=out_ref.at[c, 1], dst_ref=out_ref.at[c, 2 * way],
+            send_sem=lsend.at[c, way], recv_sem=lrecv.at[c, way],
+            device_id=(lat, left if way else right), device_id_type=MESH)
+
+    def relay(c, s):
+        swap(c, s).wait_recv()
+
+        @pl.when(hands_on)
+        def _():
+            hand(c, s).start()
+
+    for c in range(chunks):
+        for s in range(pieces):
+            swap(c, s).start()
+    for c in range(chunks):
+        ext[c, size:2 * size] = x_ref[c]
+
+    @pl.when(jnp.logical_not(gets))
+    def _():
+        for c in range(chunks):
+            ext[c, pl.ds(pl.multiple_of(far, 8), size)] = jnp.zeros((size, LANES), jnp.float32)
+
+    rows_lat = size // cols
+    classes = 1
+    while classes * cols % 8:
+        classes *= 2
+    block = classes * cols
+    order = [(c, s) for c in range(chunks) for s in range(pieces)]
+    at = 0
+    for c in range(chunks):
+        ahead = min(len(order), (c + 1) * pieces + pieces // 2)
+        for p in order[at:ahead]:
+            relay(*p)
+        at = ahead
+
+        @pl.when(gets)
+        def _():
+            for s in range(pieces):
+                hand(c, s).wait_recv()
+
+        for q in range(1, classes):
+            shifted[q - 1, :3 * size - q * cols] = ext[c, q * cols:]
+
+        def smooth(b, carry):
+            acc = None
+            for k in range(taps):
+                place = k + rows_lat - taps // 2
+                q = place % classes
+                rows = pl.ds(pl.multiple_of(b * block + (place - q) * cols, 8), block)
+                value = ext[c, rows] if q == 0 else shifted[q - 1, rows]
+                acc = w_ref[k] * value if acc is None else acc + w_ref[k] * value
+            out_ref[c, 1, pl.ds(pl.multiple_of(b * block, 8), block)] = acc
+            return carry
+
+        lax.fori_loop(0, size // block, smooth, 0)
+        side(c, 0).start()
+        side(c, 1).start()
+    for c in range(chunks):
+        for s in range(pieces):
+            swap(c, s).wait_send()
+
+    @pl.when(hands_on)
+    def _():
+        for c in range(chunks):
+            for s in range(pieces):
+                hand(c, s).wait_send()
+
+    for c in range(chunks):
+        side(c, 0).wait()
+        side(c, 1).wait()
+
+
+def halo(tiles, lat_kernel, cols):
+    n_lat, n_lon = lax.axis_size("lat"), lax.axis_size("lon")
+    chunks, size, width = tiles.shape
+    classes = 1
+    while classes * cols % 8:
+        classes *= 2
+    pieces = next(p for p in (5, 4, 2, 1) if size % (8 * p) == 0)
+    dma = pltpu.SemaphoreType.DMA
+    vmem = pl.BlockSpec(memory_space=pltpu.VMEM)
+    return pl.pallas_call(
+        functools.partial(halo_kernel, n_lat, n_lon, cols, lat_kernel.shape[0], pieces),
+        out_shape=jax.ShapeDtypeStruct((chunks, 3, size, width), jnp.float32),
+        in_specs=[vmem, pl.BlockSpec(memory_space=pltpu.SMEM)],
+        out_specs=vmem,
+        scratch_shapes=[
+            pltpu.VMEM((chunks, 3 * size, width), jnp.float32),
+            pltpu.VMEM((max(1, classes - 1), 3 * size, width), jnp.float32),
+        ] + [dma((chunks, pieces))] * 4 + [dma((chunks, 2))] * 2,
+        compiler_params=pltpu.CompilerParams(collective_id=1, has_side_effects=True),
+        name="halo",
+    )(tiles, lat_kernel)
+
+
+def gram_kernel(cols, group, x_ref, lon_ref, w_ref, m_ref, g_ref):
+    chunks, parts, size, width = x_ref.shape
+    taps = lon_ref.shape[0]
+    rows = group * cols
+    shape = (rows, parts * rows)
+    r, e = lax.broadcasted_iota(jnp.int32, shape, 0), lax.broadcasted_iota(jnp.int32, shape, 1)
+    part = sum((e >= p * rows).astype(jnp.int32) for p in range(1, parts)) + jnp.zeros(shape, jnp.int32)
+    e = e - part * rows
+    er = sum((e >= q * cols).astype(jnp.int32) for q in range(1, group)) + jnp.zeros(shape, jnp.int32)
+    rr = sum((r >= q * cols).astype(jnp.int32) for q in range(1, group)) + jnp.zeros(shape, jnp.int32)
+    offset = part * cols + (e - er * cols) - (r - rr * cols) - (cols - taps // 2)
+    offset = jnp.where(er == rr, offset, -1)
+    band = jnp.zeros(shape, jnp.float32)
+    for k in range(taps):
+        band = jnp.where(offset == k, lon_ref[k], band)
+    which = rr[:, :1] + jnp.zeros((rows, chunks * width), jnp.int32)
+    for g in range(size // rows):
+        at = slice(g * rows, (g + 1) * rows)
+        value = jnp.concatenate(
+            [jnp.concatenate([x_ref[c, p, at] for c in range(chunks)], axis=1) for p in range(parts)], axis=0)
+        value = jnp.dot(band, value, precision=lax.Precision.HIGHEST, preferred_element_type=jnp.float32)
+        weight = jnp.zeros(value.shape, jnp.float32)
+        for q in range(group):
+            weight = jnp.where(which == q, w_ref[g * group + q], weight)
+        m_ref[at] = value * weight
+    g_ref[...] = lax.dot_general(
+        m_ref[...], m_ref[...], (((0,), (0,)), ((), ())),
+        precision=lax.Precision.HIGHEST, preferred_element_type=jnp.float32)
+
+
+def matrix_and_gram(ext, lon_kernel, weights, cols):
+    chunks, parts, size, width = ext.shape
+    rows_lat = size // cols
+    group = max(q for q in range(1, rows_lat + 1) if rows_lat % q == 0 and q * cols % 8 == 0 and (q * cols <= 96 or q == rows_lat))
+    group = min([q for q in range(1, rows_lat + 1) if rows_lat % q == 0 and q * cols % 8 == 0 and 64 <= q * cols] or [group])
+    vmem, smem = pl.BlockSpec(memory_space=pltpu.VMEM), pl.BlockSpec(memory_space=pltpu.SMEM)
+    steps = chunks * width
+    return pl.pallas_call(
+        functools.partial(gram_kernel, cols, group),
+        out_shape=(jax.ShapeDtypeStruct((size, steps), jnp.float32), jax.ShapeDtypeStruct((steps, steps), jnp.float32)),
+        in_specs=[vmem, smem, smem],
+        out_specs=(vmem, vmem),
+        name="matrix_gram",
+    )(ext, lon_kernel, weights)
+
+
 def body(field, lat_kernel, lon_kernel, time_taps):
     rows_lat, rows_lon, length_in = field.shape
     steps_out = length_in - 2 * TH
@@ -215,36 +373,22 @@
     centre = (jnp.arange(2 * TH + 1, dtype=jnp.int32) == TH).astype(jnp.float32)
     taps_full = time_taps + centre
     skew_time = skewed(taps_full, steps_out, length_in)
-    filtered = lax.dot_general(
-        field.reshape(-1, length_in),
-        skew_time,
-        (((1,), (1,)), ((), ())),
-        precision=lax.Precision.HIGHEST,
-        preferred_element_type=jnp.float32,
-    ).reshape(rows_lat, rows_lon, steps_out)
-    lat_band = banded(lat_kernel, rows_lat)
-    lon_band = banded(lon_kernel, rows_lon)
-    extended = extended_2(filtered, (("lat", 0),), SH, False)
-    narrow = smooth_rows(lat_band, extended)
-    lat_done = extended_2(narrow, (("lon", 1),), SH, True)
-    smooth = jnp.einsum(
-        "jk,ikt->ijt",
-        lon_band,
-        lat_done,
-        precision=lax.Precision.HIGHEST,
-        preferred_element_type=jnp.float32,
-    )
+    flat = field.reshape(-1, length_in)
+    tiles = jnp.stack([
+        lax.dot_general(
+            flat,
+            skew_time[at:at + LANES],
+            (((1,), (1,)), ((), ())),
+            precision=lax.Precision.HIGHEST,
+            preferred_element_type=jnp.float32,
+        )
+        for at in range(0, steps_out, LANES)
+    ])
+    ext = halo(tiles, lat_kernel, rows_lon)
     globrow = (lat_place * rows_lat + jnp.arange(rows_lat, dtype=jnp.int32)).astype(jnp.float32)
     latitude = jnp.pi * (globrow + 0.5) / total_lat - jnp.pi / 2
     weights = jnp.sqrt(jnp.cos(latitude))
-    matrix = (smooth * weights[:, None, None]).reshape(-1, steps_out)
-    local_gram = lax.dot_general(
-        matrix,
-        matrix,
-        (((0,), (0,)), ((), ())),
-        precision=lax.Precision.HIGHEST,
-        preferred_element_type=jnp.float32,
-    )
+    matrix, local_gram = matrix_and_gram(ext, lon_kernel, weights, rows_lon)
     gram = sum_over_mesh(local_gram)
     upper, inverse = factor(gram, float(cells) ** 0.5)
     basis = lax.dot_general(

time: 81 us -> 68.4 us (0.84)
  Pallas kernels: 39.8 us -> 60.3 us
  waiting for transfers between devices: 19.2 us -> 0 us
  starting transfers between devices: 10.4 us -> 0 us
  matrix products: 7.14 us -> 2.92 us
  other arithmetic: 0.99 us -> 2.11 us
    pallas_call x0 -> x2, Pallas kernels: none -> 28.4 us  [the longest x1 24.7 us: halo(): pl.pallas_call(functools.partial(halo_kernel, n_lat, n_lon, cols, lat_ker...]
    ppermute x4 -> x0, waiting for transfers between devices: 19.2 us -> none  [the longest x2 10 us: extended_2(): after = lax.ppermute(initial, axis, down)]
    ppermute x4 -> x0, starting transfers between devices: 10.4 us -> none  [the longest x2 5.59 us: extended_2(): before = lax.ppermute(last, axis, up)]
    pallas_call x1, Pallas kernels: 28.6 us -> 20.6 us  [sum_over_mesh(): pl.pallas_call(functools.partial(sum_kernel, n_lat, n_lon, pair), out_sha...]
    dot_general x4 -> x2, matrix products: 4.82 us -> 1.33 us  [body(): lax.dot_general(flat, skew_time[at:at + LANES], (((1,), (1,)), ((), ())),...]
  transfers between devices with their start and end apart: 4 -> 0, of which waited for: 4 -> 0; matrix products, arithmetic and copies ran while one was open for 1% -> 0% of each run, Pallas kernels for 0% -> 0%
where the time goes in v2:
time: 68.4 us; the launch traced here: 68.1 us
  Pallas kernels  60.3 us (88%)
  matrix products  2.92 us (4%)
  other arithmetic  2.11 us (3%)
  local copies, waits for them, and re-layouts  2.02 us (3%)
  between operations  0.73 us (1%)
    pallas_call x1, Pallas kernels, halo(): pl.pallas_call(functools.partial(halo_kernel, n_lat, n_lon, cols, lat_ker...  24.7 us
    pallas_call x1, Pallas kernels, sum_over_mesh(): pl.pallas_call(functools.partial(sum_kernel, n_lat, n_lon, pair), out_sha...  20.6 us
    pallas_call x1, Pallas kernels, factor(): pl.pallas_call(functools.partial(factor_kernel, scale), out_shape=(shape,...  11.3 us
    pallas_call x1, Pallas kernels, matrix_and_gram(): pl.pallas_call(functools.partial(gram_kernel, cols, group), out_shape=(ja...  3.72 us
    dot_general x1, matrix products, body(): lax.dot_general(matrix, inverse, (((1,), (1,)), ((), ())), precision=lax....  1.6 us

profile of v2, /device:TPU:0, one launch (start us, length us, event | category | flops | bytes accessed | tf_op | source)
XLA Modules:
  0.0 68.1 jit_solution(5440060671982744105)
XLA Ops:
  0.6 0.7 cosine_sqrt_fusion.w_ref
  1.3 0.7 %fusion = f32[129]{0:T(256)S(1)} fusion(f32[129]{0:T(256)} %param.7), kind=kLoop, calls=%fused_computation.4 | loop fusion | flops 387 | bytes 1032 | tf_op jit(solution)/shard_map/add | solution.py:374
  2.0 0.1 tile.4
  2.0 0.0 copy-start
  2.0 0.5 tile.10
  2.7 0.5 copy-done
  3.2 0.1 reshape.18
  3.2 0.7 convolution_bitcast_fusion
  3.9 0.7 convolution_bitcast_fusion.1
  4.6 0.8 %pad_maximum_fusion.x_ref = f32[2,400,128]{2,1,0:T(8,128)} fusion(f32[1,400,128]{2,1,0:T(8,128)S(1)} %convolution_bitcast_fusion, f32[1,400,128]{2,1,0:T(8,128)S(1)} %convolution_bitcast_fusion.1), kind=kLoop, calls=%fused_computation.2 | loop fusion | flops 102400 | bytes 819200 | tf_op jit(solution)/shard_map/stack | solution.py:377
  5.3 24.7 %halo.1.x_ref = f32[2,3,400,128]{3,2,1,0:T(8,128)} custom-call(f32[2,400,128]{2,1,0:T(8,128)} %pad_maximum_fusion.x_ref, f32[41]{0:T(128)} %w_ref.1), custom_call_target="tpu_custom_call" | custom-call | tf_op jit(solution)/shard_map/halo/pallas_call | solution.py:307
  30.1 3.7 %matrix_gram.1 = (f32[400,256]{1,0:T(8,128)}, f32[256,256]{1,0:T(8,128)}) custom-call(f32[2,3,400,128]{3,2,1,0:T(8,128)} %halo.1.x_ref, f32[41]{0:T(128)} %lon_ref.1, f32[20]{0:T(128)} %cosine_sqrt_fusion.w_ref), custom_call_target="tpu_custom_call" | custom-call | tf_op jit(solution)/shard_map/matrix_gram/pallas_call | solution.py:358
  33.8 20.6 %gram_sum.1.g_ref = f32[256,256]{1,0:T(8,128)} custom-call(f32[256,256]{1,0:T(8,128)} %get-tuple-element.7.g_ref), custom_call_target="tpu_custom_call" | custom-call | tf_op jit(solution)/shard_map/gram_sum/pallas_call | solution.py:96
  54.4 11.3 %factor.1 = (f32[256,256]{1,0:T(8,128)}, f32[256,256]{1,0:T(8,128)}) custom-call(f32[256,256]{1,0:T(8,128)} %gram_sum.1.g_ref), custom_call_target="tpu_custom_call" | custom-call | tf_op jit(solution)/shard_map/factor/pallas_call | solution.py:173
  65.7 1.6 %fusion.2 = f32[400,256]{1,0:T(8,128)S(1)} fusion(f32[400,256]{1,0:T(8,128)} %get-tuple-element.6, f32[256,256]{1,0:T(8,128)} %get-tuple-element.8), kind=kOutput, calls=%fused_computation.7 | convolution fusion | flops 314572800 | bytes 1081344 | tf_op jit(solution)/shard_map/dot_general | solution.py:394
  67.3 0.8 %reshape.19 = f32[20,20,256]{2,1,0:T(8,128)} reshape(f32[400,256]{1,0:T(8,128)S(1)} %fusion.2) | data formatting | bytes 819200 | tf_op jit(solution)/shard_map/reshape | solution.py:400
  (4 shorter events, 0.1 us)
Async XLA Ops:
  2.0 1.1 %copy-start = (f32[20,20,384]{2,1,0:T(8,128)S(1)}, f32[20,20,384]{2,1,0:T(8,128)}, u32[]{:S(2)}) copy-start(f32[20,20,384]{2,1,0:T(8,128)} %param.4) | copy-start | bytes 1843204

commit v3 on v2

--- a/solution.py
+++ b/solution.py
@@ -2,19 +2,11 @@
 
 import jax
 import jax.numpy as jnp
+import numpy as np
 from jax import lax
 from jax.experimental import pallas as pl
 from jax.experimental.pallas import tpu as pltpu
 from jax.sharding import PartitionSpec as P
-
-TH = 64
-SH = 20
-
-
-def skewed(coeffs, count, width):
-    period = jnp.pad(coeffs, (0, count))
-    flat = jnp.tile(period, count)[: count * width]
-    return flat.reshape(count, width)
 
 
 MESH = pl.DeviceIdType.MESH
@@ -108,9 +100,14 @@
     )(gram)
 
 
-def factor_kernel(scale, g_ref, r_ref, y_ref, a, b):
-    n = g_ref.shape[0]
-    a[...] = g_ref[...]
+def factor_kernel(scale, n, g_ref, m_ref, r_ref, basis_ref, a, b, y_ref):
+    at = 0
+    for t in range(0, n, LANES):
+        if t:
+            a[t:t + LANES, :t] = jnp.zeros((LANES, t), jnp.float32)
+        for q in range(t, n, LANES):
+            a[t:t + LANES, q:q + LANES] = g_ref[at:at + LANES]
+            at += LANES
     b[...] = (lax.broadcasted_iota(jnp.int32, (n, n), 0) == lax.broadcasted_iota(jnp.int32, (n, n), 1)).astype(jnp.float32)
     sub = lax.broadcasted_iota(jnp.int32, (8, LANES), 0)
     tiles = n // LANES
@@ -164,20 +161,59 @@
             w_a = n - nt * LANES
             a[nxt:, nt * LANES:] = a[nxt:, nt * LANES:] - upd[:, :w_a]
             b[nxt:, :(kt + 1) * LANES] = b[nxt:, :(kt + 1) * LANES] - upd[:, w_a:]
-
-
-def factor(gram, scale):
-    n = gram.shape[0]
-    shape = jax.ShapeDtypeStruct((n, n), jnp.float32)
+        if nxt % LANES == 0:
+            at = kt * LANES
+            part = lax.dot_general(
+                m_ref[:, :nxt], y_ref[at:nxt, :nxt], (((1,), (1,)), ((), ())),
+                precision=lax.Precision.HIGHEST, preferred_element_type=jnp.float32)
+            cols = basis_ref.shape[1]
+            for i in range(basis_ref.shape[0]):
+                basis_ref[i, :, at:nxt] = part[i * cols:(i + 1) * cols]
+
+
+def factor(gram, matrix, scale, rows, cols):
+    n = matrix.shape[1]
+    square = jax.ShapeDtypeStruct((n, n), jnp.float32)
     vmem = pl.BlockSpec(memory_space=pltpu.VMEM)
     return pl.pallas_call(
-        functools.partial(factor_kernel, scale),
-        out_shape=(shape, shape),
-        in_specs=[vmem],
+        functools.partial(factor_kernel, scale, n),
+        out_shape=(square, jax.ShapeDtypeStruct((rows, cols, n), jnp.float32)),
+        in_specs=[vmem, vmem],
         out_specs=(vmem, vmem),
-        scratch_shapes=[pltpu.VMEM((n, n), jnp.float32)] * 2,
+        scratch_shapes=[pltpu.VMEM((n, n), jnp.float32)] * 3,
         name="factor",
-    )(gram)
+    )(gram, matrix)
+
+
+def filter_kernel(taps, v_ref, x_ref, out_ref, flat):
+    rows, cols, length = x_ref.shape
+    chunks = out_ref.shape[0]
+    steps = chunks * LANES
+    for i in range(rows):
+        flat[i * cols:(i + 1) * cols] = x_ref[i]
+    lane = lax.broadcasted_iota(jnp.int32, (1, length), 1)
+    row = jnp.where(lane == taps // 2, v_ref[...] + 1.0, v_ref[...])
+    band = pltpu.roll(jnp.broadcast_to(row, (steps, length)), 0, 1, stride=1, stride_axis=0)
+    for c in range(chunks):
+        out_ref[c] = lax.dot_general(
+            flat[...], band[c * LANES:(c + 1) * LANES], (((1,), (1,)), ((), ())),
+            precision=lax.Precision.HIGHEST, preferred_element_type=jnp.float32)
+
+
+def filtered_tiles(field, time_taps):
+    rows, cols, length = field.shape
+    taps = time_taps.shape[0]
+    chunks = (length - taps + 1) // LANES
+    row = jnp.pad(time_taps, (0, length - taps)).reshape(1, length)
+    vmem = pl.BlockSpec(memory_space=pltpu.VMEM)
+    return pl.pallas_call(
+        functools.partial(filter_kernel, taps),
+        out_shape=jax.ShapeDtypeStruct((chunks, rows * cols, LANES), jnp.float32),
+        in_specs=[vmem, vmem],
+        out_specs=vmem,
+        scratch_shapes=[pltpu.VMEM((rows * cols, length), jnp.float32)],
+        name="filter",
+    )(row, field)
 
 
 def halo_kernel(n_lat, n_lon, cols, taps, pieces, x_ref, w_ref, out_ref, ext, shifted, psend, precv, fsend, frecv, lsend, lrecv):
@@ -322,6 +358,7 @@
     chunks, parts, size, width = x_ref.shape
     taps = lon_ref.shape[0]
     rows = group * cols
+    first_row = lax.axis_index("lat") * (size // cols)
     shape = (rows, parts * rows)
     r, e = lax.broadcasted_iota(jnp.int32, shape, 0), lax.broadcasted_iota(jnp.int32, shape, 1)
     part = sum((e >= p * rows).astype(jnp.int32) for p in range(1, parts)) + jnp.zeros(shape, jnp.int32)
@@ -341,11 +378,18 @@
         value = jnp.dot(band, value, precision=lax.Precision.HIGHEST, preferred_element_type=jnp.float32)
         weight = jnp.zeros(value.shape, jnp.float32)
         for q in range(group):
-            weight = jnp.where(which == q, w_ref[g * group + q], weight)
+            weight = jnp.where(which == q, w_ref[first_row + g * group + q], weight)
         m_ref[at] = value * weight
-    g_ref[...] = lax.dot_general(
-        m_ref[...], m_ref[...], (((0,), (0,)), ((), ())),
-        precision=lax.Precision.HIGHEST, preferred_element_type=jnp.float32)
+    steps = chunks * width
+    at = 0
+    for t in range(0, steps, LANES):
+        left = m_ref[:, t:t + LANES]
+        both = lax.dot_general(
+            left, m_ref[:, t:], (((0,), (0,)), ((), ())),
+            precision=lax.Precision.HIGHEST, preferred_element_type=jnp.float32)
+        for q in range(0, steps - t, LANES):
+            g_ref[at:at + LANES] = both[:, q:q + LANES]
+            at += LANES
 
 
 def matrix_and_gram(ext, lon_kernel, weights, cols):
@@ -355,9 +399,11 @@
     group = min([q for q in range(1, rows_lat + 1) if rows_lat % q == 0 and q * cols % 8 == 0 and 64 <= q * cols] or [group])
     vmem, smem = pl.BlockSpec(memory_space=pltpu.VMEM), pl.BlockSpec(memory_space=pltpu.SMEM)
     steps = chunks * width
+    tiles = steps // LANES
+    packed = LANES * tiles * (tiles + 1) // 2
     return pl.pallas_call(
         functools.partial(gram_kernel, cols, group),
-        out_shape=(jax.ShapeDtypeStruct((size, steps), jnp.float32), jax.ShapeDtypeStruct((steps, steps), jnp.float32)),
+        out_shape=(jax.ShapeDtypeStruct((size, steps), jnp.float32), jax.ShapeDtypeStruct((packed, LANES), jnp.float32)),
         in_specs=[vmem, smem, smem],
         out_specs=(vmem, vmem),
         name="matrix_gram",
@@ -365,39 +411,16 @@
 
 
 def body(field, lat_kernel, lon_kernel, time_taps):
-    rows_lat, rows_lon, length_in = field.shape
-    steps_out = length_in - 2 * TH
-    lat_place = lax.axis_index("lat")
+    rows_lat, rows_lon = field.shape[:2]
     total_lat = rows_lat * lax.axis_size("lat")
     cells = total_lat * rows_lon * lax.axis_size("lon")
-    centre = (jnp.arange(2 * TH + 1, dtype=jnp.int32) == TH).astype(jnp.float32)
-    taps_full = time_taps + centre
-    skew_time = skewed(taps_full, steps_out, length_in)
-    flat = field.reshape(-1, length_in)
-    tiles = jnp.stack([
-        lax.dot_general(
-            flat,
-            skew_time[at:at + LANES],
-            (((1,), (1,)), ((), ())),
-            precision=lax.Precision.HIGHEST,
-            preferred_element_type=jnp.float32,
-        )
-        for at in range(0, steps_out, LANES)
-    ])
+    tiles = filtered_tiles(field, time_taps)
     ext = halo(tiles, lat_kernel, rows_lon)
-    globrow = (lat_place * rows_lat + jnp.arange(rows_lat, dtype=jnp.int32)).astype(jnp.float32)
-    latitude = jnp.pi * (globrow + 0.5) / total_lat - jnp.pi / 2
-    weights = jnp.sqrt(jnp.cos(latitude))
+    latitude = np.pi * (np.arange(total_lat) + 0.5) / total_lat - np.pi / 2
+    weights = jnp.asarray(np.sqrt(np.cos(latitude)), jnp.float32)
     matrix, local_gram = matrix_and_gram(ext, lon_kernel, weights, rows_lon)
     gram = sum_over_mesh(local_gram)
-    upper, inverse = factor(gram, float(cells) ** 0.5)
-    basis = lax.dot_general(
-        matrix,
-        inverse,
-        (((1,), (1,)), ((), ())),
-        precision=lax.Precision.HIGHEST,
-        preferred_element_type=jnp.float32,
-    ).reshape(rows_lat, rows_lon, steps_out)
+    upper, basis = factor(gram, matrix, float(cells) ** 0.5, rows_lat, rows_lon)
     return (basis, upper)
 
 

time: 68.4 us -> 64.9 us (0.949)
  matrix products: 2.92 us -> 0 us
  Pallas kernels: 60.3 us -> 62.8 us
  other arithmetic: 2.11 us -> 0 us
  local copies, waits for them, and re-layouts: 2.02 us -> 1.25 us
    pallas_call x1 -> x2, Pallas kernels: 11.3 us -> 15.1 us  [the longest x1 11.9 us: factor(): pl.pallas_call(functools.partial(factor_kernel, scale, n), out_shape=(squ...]
    dot_general x3 -> x0, matrix products: 2.92 us -> none  [the longest x1 1.6 us: body(): lax.dot_general(matrix, inverse, (((1,), (1,)), ((), ())), precision=lax....]
    pallas_call x1, Pallas kernels: 20.6 us -> 19.4 us  [sum_over_mesh(): pl.pallas_call(functools.partial(sum_kernel, n_lat, n_lon, pair), out_sha...]
    another operation x1 -> x0, other arithmetic: 0.78 us -> none  [body(): jnp.stack([lax.dot_general(flat, skew_time[at:at + LANES], (((1,), (1,)),...]
where the time goes in v3:
time: 64.9 us; the launch traced here: 64.7 us
  Pallas kernels  62.8 us (97%)
  local copies, waits for them, and re-layouts  1.25 us (2%)
  between operations  0.65 us (1%)
    pallas_call x1, Pallas kernels, halo(): pl.pallas_call(functools.partial(halo_kernel, n_lat, n_lon, cols, lat_ker...  24.7 us
    pallas_call x1, Pallas kernels, sum_over_mesh(): pl.pallas_call(functools.partial(sum_kernel, n_lat, n_lon, pair), out_sha...  19.4 us
    pallas_call x1, Pallas kernels, factor(): pl.pallas_call(functools.partial(factor_kernel, scale, n), out_shape=(squ...  11.9 us
    pallas_call x1, Pallas kernels, matrix_and_gram(): pl.pallas_call(functools.partial(gram_kernel, cols, group), out_shape=(ja...  3.59 us
    pallas_call x1, Pallas kernels, filtered_tiles(): pl.pallas_call(functools.partial(filter_kernel, taps), out_shape=jax.Shap...  3.14 us

profile of v3, /device:TPU:0, one launch (start us, length us, event | category | flops | bytes accessed | tf_op | source)
XLA Modules:
  0.0 64.7 jit_solution(7809880611336551491)
XLA Ops:
  0.6 0.7 %pad.4 = f32[384]{0:T(512)S(1)} pad(f32[129]{0:T(256)} %param.8, f32[]{:T(128)} %constant.4.clone.1), padding=0_255 | pad | bytes 2056 | tf_op jit(solution)/shard_map/jit(_pad)/pad | solution.py:207
  1.3 0.6 reshape.7.v_ref
  1.9 3.1 %filter.1.x_ref = f32[2,400,128]{2,1,0:T(8,128)} custom-call(f32[1,384]{1,0:T(1,128)} %reshape.7.v_ref, f32[20,20,384]{2,1,0:T(8,128)} %x_ref.1), custom_call_target="tpu_custom_call" | custom-call | tf_op jit(solution)/shard_map/filter/pallas_call | solution.py:209
  5.0 24.7 %halo.1.x_ref = f32[2,3,400,128]{3,2,1,0:T(8,128)} custom-call(f32[2,400,128]{2,1,0:T(8,128)} %filter.1.x_ref, f32[41]{0:T(128)} %w_ref.2), custom_call_target="tpu_custom_call" | custom-call | tf_op jit(solution)/shard_map/halo/pallas_call | solution.py:343
  29.7 3.6 %matrix_gram.1 = (f32[400,256]{1,0:T(8,128)}, f32[384,128]{1,0:T(8,128)}) custom-call(f32[2,3,400,128]{3,2,1,0:T(8,128)} %halo.1.x_ref, f32[41]{0:T(128)} %lon_ref.1, f32[80]{0:T(128)} %constant.5.clone.w_ref), custom_call_target="tpu_custom_call" | custom-call | tf_op jit(solution)/shard_map/matrix_gram/pallas_call | solution.py:404
  33.3 19.4 %gram_sum.1.g_ref = f32[384,128]{1,0:T(8,128)} custom-call(f32[384,128]{1,0:T(8,128)} %get-tuple-element.6.g_ref), custom_call_target="tpu_custom_call" | custom-call | tf_op jit(solution)/shard_map/gram_sum/pallas_call | solution.py:88
  52.8 11.9 %factor.1 = (f32[256,256]{1,0:T(8,128)}, f32[20,20,256]{2,1,0:T(8,128)}) custom-call(f32[384,128]{1,0:T(8,128)} %gram_sum.1.g_ref, f32[400,256]{1,0:T(8,128)} %get-tuple-element.7.m_ref), custom_call_target="tpu_custom_call" | custom-call | tf_op jit(solution)/shard_map/factor/pallas_call | solution.py:178

commit v4 on v3

--- a/solution.py
+++ b/solution.py
@@ -14,7 +14,7 @@
 LANES = 128
 
 
-def sum_kernel(n_lat, n_lon, pair, g_ref, out_ref, rbuf, zbuf, ssem, rsem, zssem, zrsem, cssem, crsem):
+def sum_kernel(n_lat, n_lon, pair, cols, group, x_ref, lon_ref, w_ref, m_ref, out_ref, g_ref, rbuf, zbuf, ssem, rsem, zssem, zrsem, cssem, crsem):
     lat, lon = lax.axis_index("lat"), lax.axis_index("lon")
     n_p, n_z = n_lat * pair, n_lon // pair
     rows = g_ref.shape[0] // n_p
@@ -33,6 +33,7 @@
         pl.semaphore_signal(barrier, inc=1, device_id=plane_peer(o)[1], device_id_type=MESH)
     for o in range(1, n_z):
         pl.semaphore_signal(barrier, inc=1, device_id=z_peer(o), device_id_type=MESH)
+    gram_kernel(cols, group, x_ref, lon_ref, w_ref, m_ref, g_ref)
     pl.semaphore_wait(barrier, n_p + n_z - 2)
 
     copies = []
@@ -75,29 +76,6 @@
         copies.append(c)
     for c in copies:
         c.wait()
-
-
-def sum_over_mesh(gram):
-    n_lat, n_lon = lax.axis_size("lat"), lax.axis_size("lon")
-    pair = 2 if n_lon % 2 == 0 else 1
-    n_p, n_z = n_lat * pair, n_lon // pair
-    if gram.shape[0] % (8 * n_p):
-        return lax.psum(gram, ("lat", "lon"))
-    rows, width = gram.shape[0] // n_p, gram.shape[1]
-    dma = pltpu.SemaphoreType.DMA
-    return pl.pallas_call(
-        functools.partial(sum_kernel, n_lat, n_lon, pair),
-        out_shape=jax.ShapeDtypeStruct(gram.shape, jnp.float32),
-        in_specs=[pl.BlockSpec(memory_space=pltpu.VMEM)],
-        out_specs=pl.BlockSpec(memory_space=pltpu.VMEM),
-        scratch_shapes=[
-            pltpu.VMEM((n_p, rows, width), jnp.float32),
-            pltpu.VMEM((n_z, rows, width), jnp.float32),
-            dma((n_p,)), dma((n_p,)), dma((n_z,)), dma((n_z,)), dma((n_p,)), dma((n_p,)),
-        ],
-        compiler_params=pltpu.CompilerParams(collective_id=0, has_side_effects=True),
-        name="gram_sum",
-    )(gram)
 
 
 def factor_kernel(scale, n, g_ref, m_ref, r_ref, basis_ref, a, b, y_ref):
@@ -185,14 +163,16 @@
     )(gram, matrix)
 
 
-def filter_kernel(taps, v_ref, x_ref, out_ref, flat):
+def filter_kernel(taps, v_ref, x_ref, out_ref, flat, row_ref):
     rows, cols, length = x_ref.shape
     chunks = out_ref.shape[0]
     steps = chunks * LANES
     for i in range(rows):
         flat[i * cols:(i + 1) * cols] = x_ref[i]
     lane = lax.broadcasted_iota(jnp.int32, (1, length), 1)
-    row = jnp.where(lane == taps // 2, v_ref[...] + 1.0, v_ref[...])
+    row_ref[...] = jnp.zeros((1, length), jnp.float32)
+    row_ref[:, :taps] = v_ref[...].reshape(1, taps)
+    row = jnp.where(lane == taps // 2, row_ref[...] + 1.0, row_ref[...])
     band = pltpu.roll(jnp.broadcast_to(row, (steps, length)), 0, 1, stride=1, stride_axis=0)
     for c in range(chunks):
         out_ref[c] = lax.dot_general(
@@ -204,16 +184,15 @@
     rows, cols, length = field.shape
     taps = time_taps.shape[0]
     chunks = (length - taps + 1) // LANES
-    row = jnp.pad(time_taps, (0, length - taps)).reshape(1, length)
     vmem = pl.BlockSpec(memory_space=pltpu.VMEM)
     return pl.pallas_call(
         functools.partial(filter_kernel, taps),
         out_shape=jax.ShapeDtypeStruct((chunks, rows * cols, LANES), jnp.float32),
         in_specs=[vmem, vmem],
         out_specs=vmem,
-        scratch_shapes=[pltpu.VMEM((rows * cols, length), jnp.float32)],
+        scratch_shapes=[pltpu.VMEM((rows * cols, length), jnp.float32), pltpu.VMEM((1, length), jnp.float32)],
         name="filter",
-    )(row, field)
+    )(time_taps, field)
 
 
 def halo_kernel(n_lat, n_lon, cols, taps, pieces, x_ref, w_ref, out_ref, ext, shifted, psend, precv, fsend, frecv, lsend, lrecv):
@@ -401,12 +380,24 @@
     steps = chunks * width
     tiles = steps // LANES
     packed = LANES * tiles * (tiles + 1) // 2
+    n_lat, n_lon = lax.axis_size("lat"), lax.axis_size("lon")
+    pair = 2 if n_lon % 2 == 0 else 1
+    n_p, n_z = n_lat * pair, n_lon // pair
+    share = packed // n_p
+    dma = pltpu.SemaphoreType.DMA
     return pl.pallas_call(
-        functools.partial(gram_kernel, cols, group),
+        functools.partial(sum_kernel, n_lat, n_lon, pair, cols, group),
         out_shape=(jax.ShapeDtypeStruct((size, steps), jnp.float32), jax.ShapeDtypeStruct((packed, LANES), jnp.float32)),
         in_specs=[vmem, smem, smem],
         out_specs=(vmem, vmem),
-        name="matrix_gram",
+        scratch_shapes=[
+            pltpu.VMEM((packed, LANES), jnp.float32),
+            pltpu.VMEM((n_p, share, LANES), jnp.float32),
+            pltpu.VMEM((n_z, share, LANES), jnp.float32),
+            dma((n_p,)), dma((n_p,)), dma((n_z,)), dma((n_z,)), dma((n_p,)), dma((n_p,)),
+        ],
+        compiler_params=pltpu.CompilerParams(collective_id=0, has_side_effects=True),
+        name="gram_sum",
     )(ext, lon_kernel, weights)
 
 
@@ -418,8 +409,7 @@
     ext = halo(tiles, lat_kernel, rows_lon)
     latitude = np.pi * (np.arange(total_lat) + 0.5) / total_lat - np.pi / 2
     weights = jnp.asarray(np.sqrt(np.cos(latitude)), jnp.float32)
-    matrix, local_gram = matrix_and_gram(ext, lon_kernel, weights, rows_lon)
-    gram = sum_over_mesh(local_gram)
+    matrix, gram = matrix_and_gram(ext, lon_kernel, weights, rows_lon)
     upper, basis = factor(gram, matrix, float(cells) ** 0.5, rows_lat, rows_lon)
     return (basis, upper)
 

time: 64.9 us -> 60.7 us (0.935)
  Pallas kernels: 62.8 us -> 59.9 us
  local copies, waits for them, and re-layouts: 1.25 us -> 0 us
    pallas_call x2 -> x1, Pallas kernels: 23 us -> 20.1 us  [matrix_and_gram(): pl.pallas_call(functools.partial(sum_kernel, n_lat, n_lon, pair, cols, gr...]
    pad x1 -> x0, local copies, waits for them, and re-layouts: 0.68 us -> none  [filtered_tiles(): row = jnp.pad(time_taps, (0, length - taps)).reshape(1, length)]
where the time goes in v4:
time: 60.7 us; the launch traced here: 60.5 us
  Pallas kernels  59.9 us (99%)
  between operations  0.65 us (1%)
    pallas_call x1, Pallas kernels, halo(): pl.pallas_call(functools.partial(halo_kernel, n_lat, n_lon, cols, lat_ker...  24.7 us
    pallas_call x1, Pallas kernels, matrix_and_gram(): pl.pallas_call(functools.partial(sum_kernel, n_lat, n_lon, pair, cols, gr...  20.1 us
    pallas_call x1, Pallas kernels, factor(): pl.pallas_call(functools.partial(factor_kernel, scale, n), out_shape=(squ...  11.9 us
    pallas_call x1, Pallas kernels, filtered_tiles(): pl.pallas_call(functools.partial(filter_kernel, taps), out_shape=jax.Shap...  3.15 us

profile of v4, /device:TPU:0, one launch (start us, length us, event | category | flops | bytes accessed | tf_op | source)
XLA Modules:
  0.0 60.5 jit_solution(13853333585116569471)
XLA Ops:
  0.6 3.1 %filter.1.x_ref = f32[2,400,128]{2,1,0:T(8,128)} custom-call(f32[129]{0:T(256)} %v_ref.1, f32[20,20,384]{2,1,0:T(8,128)} %x_ref.1), custom_call_target="tpu_custom_call" | custom-call | tf_op jit(solution)/shard_map/filter/pallas_call | solution.py:188
  3.8 24.7 %halo.1.x_ref = f32[2,3,400,128]{3,2,1,0:T(8,128)} custom-call(f32[2,400,128]{2,1,0:T(8,128)} %filter.1.x_ref, f32[41]{0:T(128)} %w_ref.2), custom_call_target="tpu_custom_call" | custom-call | tf_op jit(solution)/shard_map/halo/pallas_call | solution.py:322
  28.5 20.1 %gram_sum.1 = (f32[400,256]{1,0:T(8,128)}, f32[384,128]{1,0:T(8,128)}) custom-call(f32[2,3,400,128]{3,2,1,0:T(8,128)} %halo.1.x_ref, f32[41]{0:T(128)} %lon_ref.1, f32[80]{0:T(128)} %constant.2.clone.w_ref), custom_call_target="tpu_custom_call" | custom-call | tf_op jit(solution)/shard_map/gram_sum/pallas_call | solution.py:388
  48.6 11.9 %factor.1 = (f32[256,256]{1,0:T(8,128)}, f32[20,20,256]{2,1,0:T(8,128)}) custom-call(f32[384,128]{1,0:T(8,128)} %get-tuple-element.6.g_ref, f32[400,256]{1,0:T(8,128)} %get-tuple-element.7.m_ref), custom_call_target="tpu_custom_call" | custom-call | tf_op jit(solution)/shard_map/factor/pallas_call | solution.py:156
